TPU v7x, 32 devices: a whole 2x2x4 slice. The times are simulated.
32 devices in a mesh: row: 4 (over x, core), col: 8 (over z, y).
Axes of the slice: x: 2, y: 2, z: 4, core: 2. Of those that a mesh axis runs over, the one named last changes fastest.
Arguments:
- vectors: float32 [16, 4096], P(None, ('row', 'col')), may hold values from -12 to 12, as said below
- diag_energy: float32 [4096], P(('row', 'col')), may hold values from 0.5 to 4
- blocks: float32 [4, 192, 128, 128], P('row', 'col'), may hold values from -0.078125 to 0.078125
- block_row: int32 [4, 192], P('row', 'col'), may hold values from 0 to 7
- block_col: int32 [4, 192], P('row', 'col'), may hold values from 0 to 3
Outputs:
- image: float32 [16, 4096], P(None, ('row', 'col'))
- resid: float32 [16, 4096], P(None, ('row', 'col'))
Inputs may be any that keep to these rules, and one draw needn't show every extreme that they name: `vectors`: each row of X holds independent entries; the Gram matrix X X^T is positive definite.
All inputs are finite; a program needn't handle non-finite values.
Results may differ from a plain program's by a relative error of at most 0.0003.
Values sent between devices are 32-bit elements; how exact they have to be, the bound alone decides.
A program may use at most 64 MiB of HBM per device.

v0:
```python
import jax
import jax.numpy as jnp
from jax import lax
from jax.sharding import PartitionSpec as P

BLK = 128


def solve_metric(metric, gram):
    highest = lax.Precision.HIGHEST
    order = metric.shape[0]
    index = jnp.arange(order)
    factor = jnp.zeros_like(metric)
    for column in range(order):
        onehot = (index == column).astype(jnp.float32)
        rest = metric[:, column] - jnp.dot(factor, factor[column, :], precision=highest)
        pivot = jnp.sqrt(rest[column])
        values = jnp.where(index >= column, rest / pivot, 0.0)
        factor = factor + values[:, None] * onehot[None, :]
    inner = jnp.zeros_like(gram)
    for line in range(order):
        onehot = (index == line).astype(jnp.float32)
        value = (gram[line, :] - jnp.dot(factor[line, :], inner, precision=highest)) / factor[
            line, line
        ]
        inner = inner + onehot[:, None] * value[None, :]
    solved = jnp.zeros_like(gram)
    for line in range(order - 1, -1, -1):
        onehot = (index == line).astype(jnp.float32)
        value = (inner[line, :] - jnp.dot(factor[:, line], solved, precision=highest)) / factor[
            line, line
        ]
        solved = solved + onehot[:, None] * value[None, :]
    return solved


def per_device(vectors, diag_energy, blocks, block_row, block_col):
    highest = lax.Precision.HIGHEST
    count = vectors.shape[0]
    tiles = blocks[0]
    rows_here = block_row[0]
    cols_here = block_col[0]
    col_whole = lax.all_gather(vectors, "row", axis=1, tiled=True)
    row_whole = lax.all_gather(vectors, "col", axis=1, tiled=True)
    row_blocks = row_whole.shape[1] // BLK
    col_blocks = col_whole.shape[1] // BLK
    col_split = col_whole.reshape(count, col_blocks, BLK)
    row_split = row_whole.reshape(count, row_blocks, BLK)
    picked = col_split[:, cols_here]
    terms = jnp.einsum("bij,kbj->kbi", tiles, picked, precision=highest)
    onehot = (rows_here[:, None] == jnp.arange(row_blocks)[None, :]).astype(jnp.float32)
    part_one = jnp.einsum("kbi,br->kri", terms, onehot, precision=highest).reshape(
        count, row_blocks * BLK
    )
    picked_two = row_split[:, rows_here]
    terms_two = jnp.einsum("bij,kbi->kbj", tiles, picked_two, precision=highest)
    onehot_two = (cols_here[:, None] == jnp.arange(col_blocks)[None, :]).astype(jnp.float32)
    part_two = jnp.einsum("kbj,bq->kqj", terms_two, onehot_two, precision=highest).reshape(
        count, col_blocks * BLK
    )
    own_diag = diag_energy[None, :] * vectors
    metric_local = jnp.dot(
        vectors, vectors.T, precision=highest, preferred_element_type=jnp.float32
    )
    first = lax.psum_scatter(part_one, "col", scatter_dimension=1, tiled=True)
    second = lax.psum_scatter(part_two, "row", scatter_dimension=1, tiled=True)
    image = first + second + own_diag
    quad = jnp.dot(row_whole, part_one.T, precision=highest, preferred_element_type=jnp.float32)
    gram_local = (
        quad
        + quad.T
        + jnp.dot(vectors, own_diag.T, precision=highest, preferred_element_type=jnp.float32)
    )
    gram, metric = lax.psum((gram_local, metric_local), ("row", "col"))
    coef = solve_metric(metric, gram)
    resid = image - jnp.dot(coef.T, vectors, precision=highest, preferred_element_type=jnp.float32)
    return (image, resid)


def solution(mesh):
    return jax.shard_map(
        per_device,
        mesh=mesh,
        in_specs=(
            P(None, ("row", "col")),
            P(("row", "col")),
            P("row", "col", None, None),
            P("row", "col"),
            P("row", "col"),
        ),
        out_specs=(P(None, ("row", "col")), P(None, ("row", "col"))),
        check_vma=False,
    )
```

profile of v0, /device:TPU:0, one launch (start us, length us, event | category | flops | bytes accessed | tf_op | source)
XLA Modules:
  0.0 156.3 jit_solution(4022144908604003280)
XLA Ops:
  7.2 32.7 %all_gather.7 = f32[16,1024]{1,0:T(8,128)S(1)} all-gather(f32[16,128]{1,0:T(8,128)} %param.5), channel_id=1, replica_groups=mesh['row'=4,'col'=8] {'col'}, dimensions={1}, use_global_device_ids=true | all-gather | bytes 73728 | tf_op jit(solution)/shard_map/all_gather | solution.py:44
  39.9 0.7 fusion.288
  41.2 1.4 fusion.7
  42.9 0.6 copy.32
  43.6 5.2 %all_gather.6 = f32[16,512]{1,0:T(8,128)S(1)} all-gather(f32[16,128]{1,0:T(8,128)S(1)} %copy-done.1), channel_id=1, replica_groups=mesh['row'=4,'col'=8] {'row'}, dimensions={1}, use_global_device_ids=true | all-gather | bytes 40960 | tf_op jit(solution)/shard_map/all_gather | solution.py:43
  49.4 2.5 %fusion.4 = f32[16,24,128]{2,0,1:T(8,128)S(1)} fusion(f32[1,24,128,128]{3,2,1,0:T(8,128)S(1)} %copy-done, f32[24,16,128]{2,1,0:T(8,128)S(1)} %gather_fusion), kind=kOutput, calls=%fused_computation.6 | convolution fusion | flops 75497472 | bytes 1966080 | tf_op jit(solution)/shard_map/bij,kbj->kbi/dot_general | solution.py:50
  52.2 0.6 copy.31
  53.5 39.6 %all-reduce = (f32[16,16]{1,0:T(8,128)S(1)}, f32[16,16]{1,0:T(8,128)S(1)}) all-reduce(f32[16,16]{1,0:T(8,128)S(1)} %fusion.10, f32[16,16]{1,0:T(8,128)S(1)} %fusion.342), channel_id=1, replica_groups=mesh['row'=4,'col'=8] {'row','col'}, use_global_device_ids=true, to_apply=%region_2.0 | all-reduce | flops 512 | bytes 4096 | tf_op jit(solution)/shard_map/psum | solution.py:74
  94.2 0.6 slice.402
  97.8 0.6 slice.408
  99.5 0.6 slice.411
  111.7 0.6 slice.432
  113.4 0.6 slice.435
  120.0 0.7 fusion.341
  121.2 0.7 fusion.59
  121.9 0.9 fusion.60
  122.8 0.9 fusion.61
  123.7 0.8 fusion.62
  124.4 0.8 fusion.63
  125.2 0.8 fusion.64
  126.1 0.8 fusion.65
  126.9 0.8 fusion.66
  127.8 0.8 fusion.67
  128.6 0.8 fusion.68
  129.4 0.8 fusion.69
  130.2 0.8 fusion.70
  131.2 0.8 fusion.71
  132.0 0.8 fusion.72
  132.7 0.9 fusion.73
  133.6 0.9 fusion.74
  134.5 0.8 fusion.75
  135.3 0.8 fusion.76
  136.2 0.8 fusion.77
  136.9 0.9 fusion.78
  137.8 0.8 fusion.79
  138.7 0.8 fusion.80
  139.5 0.8 fusion.81
  140.3 0.9 fusion.82
  141.3 0.7 fusion.83
  142.0 0.8 fusion.84
  142.8 0.8 fusion.85
  143.6 0.8 fusion.86
  144.6 0.7 fusion.87
  145.2 0.9 fusion.88
  146.1 0.9 fusion.89
  147.0 0.8 fusion.90
  147.8 0.7 multiply_add_fusion.2
  148.5 0.9 convolution_subtract_fusion
  (119 shorter events, 16.5 us)
Async XLA Ops:
  7.2 34.0 %copy-start = (f32[1,24,128,128]{3,2,1,0:T(8,128)S(1)}, f32[1,24,128,128]{3,2,1,0:T(8,128)}, u32[]{:S(2)}) copy-start(f32[1,24,128,128]{3,2,1,0:T(8,128)} %param.7) | copy-start | bytes 4718596
  7.2 36.4 %copy-start.1 = (f32[16,128]{1,0:T(8,128)S(1)}, f32[16,128]{1,0:T(8,128)}, u32[]{:S(2)}) copy-start(f32[16,128]{1,0:T(8,128)} %param.5) | copy-start | bytes 24580
  7.2 35.5 %copy-start.4 = (s32[1,24]{1,0:T(1,128)S(1)}, s32[1,24]{1,0:T(1,128)}, u32[]{:S(2)}) copy-start(s32[1,24]{1,0:T(1,128)} %param.9) | copy-start | bytes 292
  7.2 140.6 %reduce-scatter.5.cloned.1.call-start = ((), (), s32[]{:S(2)}) async-start(), calls=%async_computation.3 | async-start | bytes 40960 | tf_op jit(solution)/shard_map/reduce_scatter | solution.py:66
  42.6 9.3 %copy-start.5 = (s32[1,24]{1,0:T(1,128)S(1)}, s32[1,24]{1,0:T(1,128)}, u32[]{:S(2)}) copy-start(s32[1,24]{1,0:T(1,128)} %param.8) | copy-start | bytes 292
  43.5 9.8 %copy-start.3 = (f32[128]{0:T(128)S(1)}, f32[128]{0:T(128)}, u32[]{:S(2)}) copy-start(f32[128]{0:T(128)} %param.6) | copy-start | bytes 1540
  43.5 104.3 %reduce-scatter.3.cloned.1.call-start = ((), (), s32[]{:S(2)}) async-start(), calls=%async_computation.2 | async-start | bytes 73728 | tf_op jit(solution)/shard_map/reduce_scatter | solution.py:65
  148.5 0.9 copy-start.2
Sparse Core Ops, SparseCore 0:
  43.6 20.4 reduce-scatter.4
  67.2 55.0 reduce-scatter.2
where the time goes:
time: 157 us; the launch traced here: 156 us
  blocking collectives  77.5 us (49%)
  matrix products  34.4 us (22%)
  between operations  25 us (16%)
  local copies, waits for them, and re-layouts  15.8 us (10%)
  other arithmetic  3.43 us (2%)
    psum x1, blocking collectives, per_device(): gram, metric = lax.psum((gram_local, metric_local), ('row', 'col'))  39.6 us
    all_gather x1, blocking collectives, per_device(): row_whole = lax.all_gather(vectors, 'col', axis=1, tiled=True)  32.7 us
    dot_general x16, matrix products, solve_metric(): jnp.dot(factor[:, line], solved, precision=highest)  13 us
    dot_general x16, matrix products, solve_metric(): jnp.dot(factor[line, :], inner, precision=highest)  13 us
    slice x15, local copies, waits for them, and re-layouts, solve_metric(): pivot = jnp.sqrt(rest[column])  8.98 us
    all_gather x1, blocking collectives, per_device(): col_whole = lax.all_gather(vectors, 'row', axis=1, tiled=True)  5.19 us
  transfers between devices with their start and end apart: 2, of which 0 were waited for; matrix products, arithmetic and copies ran while one was open for 31% of the time, Pallas kernels for 0%

commit v1 on v0

v1 whole, which is shorter than its diff:
```python
import functools

import jax
import jax.numpy as jnp
from jax import lax
from jax.experimental import pallas as pl
from jax.experimental.pallas import tpu as pltpu
from jax.sharding import PartitionSpec as P

BLK = 128
F32 = jnp.float32
BF16 = jnp.bfloat16
MESH = pl.DeviceIdType.MESH


def halves(x):
    high = x.astype(BF16)
    return high, (x - high.astype(F32)).astype(BF16)


def dot_nt(a, b):
    return lax.dot_general(a, b, (((1,), (1,)), ((), ())), preferred_element_type=F32)


def dot_nn(a, b):
    return lax.dot_general(a, b, (((1,), (0,)), ((), ())), preferred_element_type=F32)


def kernel(
    n_row, n_col,
    x_ref, diag_ref, rows_ref, cols_ref, blocks_ref,
    image_ref, resid_ref,
    tiles, split, col_x, row_x, col_lhs, row_lhs,
    met_out, met_in, p1_out, p1_in, p2_out, p2_in, g1_out, g1_in, g2_out, g2_in,
    tile_sem, cx_s, cx_r, rx_s, rx_r, m_s, m_r, p1_s, p1_r, p2_s, p2_r, g1_s, g1_r, g2_s, g2_r,
):
    count = x_ref.shape[0]
    n_blk = tiles.shape[0]
    my_row = lax.axis_index("row")
    my_col = lax.axis_index("col")

    def fan(axis, size, me, source, target, send, recv):
        copies = []
        for d in range(1, size):
            peer = lax.rem(me + d, size)
            copies.append(
                pltpu.make_async_remote_copy(
                    src_ref=source(peer), dst_ref=target(d), send_sem=send.at[d],
                    recv_sem=recv.at[d], device_id={axis: peer}, device_id_type=MESH,
                )
            )
        for copy in copies:
            copy.start()
        return copies

    fan_row = functools.partial(fan, "row", n_row, my_row)
    fan_col = functools.partial(fan, "col", n_col, my_col)

    load = pltpu.make_async_copy(blocks_ref.at[0], tiles, tile_sem)
    load.start()

    barrier = pltpu.get_barrier_semaphore()
    for d in range(1, n_col):
        pl.semaphore_signal(
            barrier, inc=1, device_id={"col": lax.rem(my_col + d, n_col)}, device_id_type=MESH
        )
    for d in range(1, n_row):
        pl.semaphore_signal(
            barrier, inc=1, device_id={"row": lax.rem(my_row + d, n_row)}, device_id_type=MESH
        )
    pl.semaphore_wait(barrier, n_row + n_col - 2)

    row_copies = fan_col(lambda peer: x_ref, lambda d: row_x.at[my_col], rx_s, rx_r)
    col_copies = fan_row(lambda peer: x_ref, lambda d: col_x.at[my_row], cx_s, cx_r)
    x_own = x_ref[...]
    row_x[my_col] = x_own
    col_x[my_row] = x_own

    load.wait()
    for b in range(n_blk):
        high, low = halves(tiles[b])
        split[b] = jnp.concatenate([high, low], axis=1)

    for copy in col_copies:
        copy.wait()
    zero = jnp.zeros((count, BLK), BF16)
    for q in range(n_row):
        high, low = halves(col_x[q])
        col_lhs[q] = jnp.concatenate(
            [jnp.concatenate([high, high], axis=1), jnp.concatenate([low, zero], axis=1)], axis=0
        )
    for copy in row_copies:
        copy.wait()
    row_two = []
    for r in range(n_col):
        high, low = halves(row_x[r])
        both = jnp.concatenate([high, low], axis=0)
        row_lhs[r] = both
        row_two.append(both)

    def fold(o):
        return o[:count, :count] + o[count:, :count] + o[:count, count:]

    x_wide = jnp.concatenate(row_two, axis=1)
    metric_part = fold(dot_nt(x_wide, x_wide))
    met_out[...] = jnp.concatenate(
        [metric_part, jnp.zeros((count, BLK - count), F32)], axis=1
    )
    met_copies = fan_row(lambda peer: met_out, lambda d: met_in.at[d], m_s, m_r)

    part_one = [jnp.zeros((count, BLK), F32) for _ in range(n_col)]
    for b in range(n_blk):
        o = dot_nt(col_lhs[cols_ref[0, b]], split[b])
        term = o[:count] + o[count:]
        place = rows_ref[0, b]
        for r in range(n_col):
            part_one[r] = part_one[r] + (place == r).astype(F32) * term
    for r in range(n_col):
        p1_out[r] = part_one[r]
    p1_copies = fan_col(lambda peer: p1_out.at[peer], lambda d: p1_in.at[d], p1_s, p1_r)

    own_diag = diag_ref[...] * x_own
    p_two = [jnp.concatenate(halves(p), axis=0) for p in part_one]
    x_two = jnp.concatenate(halves(x_own), axis=0)
    d_two = jnp.concatenate(halves(own_diag), axis=0)
    gram_part = fold(
        dot_nt(
            jnp.concatenate(row_two + p_two + [x_two], axis=1),
            jnp.concatenate(p_two + row_two + [d_two], axis=1),
        )
    )
    per = BLK // count
    groups = count // 8
    lane = lax.broadcasted_iota(jnp.int32, (count, BLK), 1)
    sub = lax.broadcasted_iota(jnp.int32, (count, BLK), 0)
    keep = (lane // count) == (sub % per)
    spread = jnp.where(keep, jnp.concatenate([gram_part] * per, axis=1), 0.0)
    g1_out[...] = jnp.concatenate(
        [jnp.sum(spread[g * per:(g + 1) * per], axis=0, keepdims=True) for g in range(groups)], axis=0
    )
    g1_copies = fan_row(lambda peer: g1_out, lambda d: g1_in.at[d], g1_s, g1_r)

    part_two = [jnp.zeros((count, BLK), F32) for _ in range(n_row)]
    for b in range(n_blk):
        o = dot_nn(row_lhs[rows_ref[0, b]], split[b])
        term = o[:count, :BLK] + o[count:, :BLK] + o[:count, BLK:]
        place = cols_ref[0, b]
        for q in range(n_row):
            part_two[q] = part_two[q] + (place == q).astype(F32) * term
    for q in range(n_row):
        p2_out[q] = part_two[q]
    p2_copies = fan_row(lambda peer: p2_out.at[peer], lambda d: p2_in.at[d], p2_s, p2_r)

    for copy in g1_copies:
        copy.wait()
    total = g1_out[...]
    for d in range(1, n_row):
        total = total + g1_in[d]
    g2_out[...] = total
    g2_copies = fan_col(lambda peer: g2_out, lambda d: g2_in.at[d], g2_s, g2_r)

    for copy in met_copies:
        copy.wait()
    metric = met_out[...]
    for d in range(1, n_row):
        metric = metric + met_in[d]
    solved = x_own
    for k in range(count):
        ratio = jnp.where(
            sub == k, 0.0,
            jnp.broadcast_to(metric[:, k:k + 1], (count, BLK))
            / jnp.broadcast_to(metric[k:k + 1, k:k + 1], (count, BLK)),
        )
        solved = solved - ratio * solved[k:k + 1]
        metric = metric - ratio * metric[k:k + 1]
    pivots = jnp.sum(jnp.where(lane == sub, metric, 0.0), axis=1, keepdims=True)
    solved = solved / pivots
    high, low = halves(solved)
    y_two = jnp.concatenate(
        [jnp.concatenate([high] * per, axis=0), jnp.concatenate([low] * per, axis=0)], axis=1
    )

    for copy in p2_copies:
        copy.wait()
    image = own_diag + p2_out[my_row]
    for d in range(1, n_row):
        image = image + p2_in[d]
    for copy in p1_copies:
        copy.wait()
    image = image + p1_out[my_col]
    for d in range(1, n_col):
        image = image + p1_in[d]
    image_ref[...] = image

    for copy in g2_copies:
        copy.wait()
    gram = g2_out[...]
    for d in range(1, n_col):
        gram = gram + g2_in[d]
    wide = jnp.concatenate(
        [jnp.broadcast_to(gram[g:g + 1], (per, BLK)) for g in range(groups)], axis=0
    )
    wide = jnp.where(keep, wide, 0.0)
    o = dot_nn(jnp.concatenate(halves(wide), axis=0), y_two)
    resid_ref[...] = image - (o[:count, :BLK] + o[count:, :BLK] + o[:count, BLK:])


def per_device(n_row, n_col, vectors, diag_energy, blocks, block_row, block_col):
    count = vectors.shape[0]
    n_blk = blocks.shape[1]
    groups = count // 8
    piece = (count, BLK)
    vmem = pl.BlockSpec(memory_space=pltpu.VMEM)
    smem = pl.BlockSpec(memory_space=pltpu.SMEM)
    dma = pltpu.SemaphoreType.DMA
    return pl.pallas_call(
        functools.partial(kernel, n_row, n_col),
        out_shape=[jax.ShapeDtypeStruct(piece, F32)] * 2,
        in_specs=[vmem, vmem, smem, smem, pl.BlockSpec(memory_space=pl.ANY)],
        out_specs=[vmem, vmem],
        scratch_shapes=[
            pltpu.VMEM((n_blk, BLK, BLK), F32),
            pltpu.VMEM((n_blk, BLK, 2 * BLK), BF16),
            pltpu.VMEM((n_row,) + piece, F32),
            pltpu.VMEM((n_col,) + piece, F32),
            pltpu.VMEM((n_row, 2 * count, 2 * BLK), BF16),
            pltpu.VMEM((n_col, 2 * count, BLK), BF16),
            pltpu.VMEM(piece, F32),
            pltpu.VMEM((n_row,) + piece, F32),
            pltpu.VMEM((n_col,) + piece, F32),
            pltpu.VMEM((n_col,) + piece, F32),
            pltpu.VMEM((n_row,) + piece, F32),
            pltpu.VMEM((n_row,) + piece, F32),
            pltpu.VMEM((groups, BLK), F32),
            pltpu.VMEM((n_row, groups, BLK), F32),
            pltpu.VMEM((groups, BLK), F32),
            pltpu.VMEM((n_col, groups, BLK), F32),
            dma,
            dma((n_row,)), dma((n_row,)),
            dma((n_col,)), dma((n_col,)),
            dma((n_row,)), dma((n_row,)),
            dma((n_col,)), dma((n_col,)),
            dma((n_row,)), dma((n_row,)),
            dma((n_row,)), dma((n_row,)),
            dma((n_col,)), dma((n_col,)),
        ],
        compiler_params=pltpu.CompilerParams(collective_id=0, has_side_effects=True),
    )(vectors, diag_energy.reshape(1, -1), block_row, block_col, blocks)


def solution(mesh):
    return jax.shard_map(
        functools.partial(per_device, mesh.shape["row"], mesh.shape["col"]),
        mesh=mesh,
        in_specs=(
            P(None, ("row", "col")),
            P(("row", "col")),
            P("row", "col", None, None),
            P("row", "col"),
            P("row", "col"),
        ),
        out_specs=(P(None, ("row", "col")), P(None, ("row", "col"))),
        check_vma=False,
    )
```

time: 157 us -> 24.5 us (0.16)
  blocking collectives: 77.5 us -> 0 us
  matrix products: 34.4 us -> 0 us
  between operations: 25 us -> 0.64 us
  Pallas kernels: 0 us -> 20.9 us
  local copies, waits for them, and re-layouts: 15.8 us -> 2.59 us
  other arithmetic: 3.43 us -> 0 us
    psum x1 -> x0, blocking collectives: 39.6 us -> none  [per_device(): gram, metric = lax.psum((gram_local, metric_local), ('row', 'col'))]
    all_gather x2 -> x0, blocking collectives: 37.9 us -> none  [the longest x1 32.7 us: per_device(): row_whole = lax.all_gather(vectors, 'col', axis=1, tiled=True)]
    dot_general x56 -> x0, matrix products: 34.4 us -> none  [the longest x16 13 us: solve_metric(): jnp.dot(factor[:, line], solved, precision=highest)]
    pallas_call x0 -> x1, Pallas kernels: none -> 20.9 us  [per_device(): pl.pallas_call(functools.partial(kernel, n_row, n_col), out_shape=[jax.Sh...]
    slice x33 -> x0, local copies, waits for them, and re-layouts: 13.3 us -> none  [the longest x15 8.98 us: solve_metric(): pivot = jnp.sqrt(rest[column])]
    add x21 -> x0, other arithmetic: 2.56 us -> none  [the longest x15 1.35 us: solve_metric(): factor = factor + values[:, None] * onehot[None, :]]
  transfers between devices with their start and end apart: 2 -> 0, of which waited for: 0 -> 0; matrix products, arithmetic and copies ran while one was open for 31% -> 0% of each run, Pallas kernels for 0% -> 0%
where the time goes in v1:
time: 24.5 us; the launch traced here: 24.1 us
  Pallas kernels  20.9 us (85%)
  local copies, waits for them, and re-layouts  2.59 us (11%)
  between operations  0.64 us (3%)
    pallas_call x1, Pallas kernels, per_device(): pl.pallas_call(functools.partial(kernel, n_row, n_col), out_shape=[jax.Sh...  20.9 us
    unnamed x2, local copies, waits for them, and re-layouts  2.59 us

profile of v1, /device:TPU:0, one launch (start us, length us, event | category | flops | bytes accessed | tf_op | source)
XLA Modules:
  0.0 24.1 jit_solution(6277425232821727075)
XLA Ops:
  0.6 20.9 %shard_map.68 = (f32[16,128]{1,0:T(8,128)}, f32[16,128]{1,0:T(8,128)}) custom-call(f32[16,128]{1,0:T(8,128)} %x_ref.1, f32[1,128]{1,0:T(1,128)} %bitcast.1, s32[1,24]{1,0:T(1,128)} %rows_ref.1, s32[1,24]{1,0:T(1,128)} %cols_ref.1, f32[1,24,128,128]{3,2,1,0:T(8,128)} %blocks_ref.1), custom_call_target="tpu_custom_call" | custom-call | tf_op jit(solution)/shard_map/pallas_call | solution.py:216
  21.5 1.3 %copy.9 = f32[16,128]{1,0:T(8,128)} copy(f32[16,128]{1,0:T(8,128)} %get-tuple-element.4) | data formatting | bytes 16384
  22.8 1.3 %copy.10 = f32[16,128]{1,0:T(8,128)} copy(f32[16,128]{1,0:T(8,128)} %get-tuple-element.5) | data formatting | bytes 16384

commit v2 on v1

--- a/solution.py
+++ b/solution.py
@@ -8,6 +8,7 @@
 from jax.sharding import PartitionSpec as P
 
 BLK = 128
+DIRECT = 64
 F32 = jnp.float32
 BF16 = jnp.bfloat16
 MESH = pl.DeviceIdType.MESH
@@ -18,6 +19,12 @@
     return high, (x - high.astype(F32)).astype(BF16)
 
 
+def add(terms):
+    while len(terms) > 1:
+        terms = [a + b for a, b in zip(terms[::2], terms[1::2])] + terms[len(terms) & ~1:]
+    return terms[0]
+
+
 def dot_nt(a, b):
     return lax.dot_general(a, b, (((1,), (1,)), ((), ())), preferred_element_type=F32)
 
@@ -28,11 +35,11 @@
 
 def kernel(
     n_row, n_col,
-    x_ref, diag_ref, rows_ref, cols_ref, blocks_ref,
-    image_ref, resid_ref,
-    tiles, split, col_x, row_x, col_lhs, row_lhs,
+    x_hbm, diag_hbm, rows_hbm, cols_hbm, blocks_hbm,
+    out_ref,
+    x_ref, diag_ref, rows_ref, cols_ref, tiles, split, col_x, row_x, col_lhs, row_lhs,
     met_out, met_in, p1_out, p1_in, p2_out, p2_in, g1_out, g1_in, g2_out, g2_in,
-    tile_sem, cx_s, cx_r, rx_s, rx_r, m_s, m_r, p1_s, p1_r, p2_s, p2_r, g1_s, g1_r, g2_s, g2_r,
+    load_sem, cx_s, cx_r, rx_s, rx_r, m_s, m_r, p1_s, p1_r, p2_s, p2_r, g1_s, g1_r, g2_s, g2_r,
 ):
     count = x_ref.shape[0]
     n_blk = tiles.shape[0]
@@ -56,8 +63,15 @@
     fan_row = functools.partial(fan, "row", n_row, my_row)
     fan_col = functools.partial(fan, "col", n_col, my_col)
 
-    load = pltpu.make_async_copy(blocks_ref.at[0], tiles, tile_sem)
-    load.start()
+    x_load, *small_loads, load = [
+        pltpu.make_async_copy(source, target, load_sem.at[at])
+        for at, (source, target) in enumerate(
+            [(x_hbm, x_ref), (diag_hbm, diag_ref), (rows_hbm, rows_ref), (cols_hbm, cols_ref),
+             (blocks_hbm.at[0], tiles)]
+        )
+    ]
+    for copy in [x_load, *small_loads, load]:
+        copy.start()
 
     barrier = pltpu.get_barrier_semaphore()
     for d in range(1, n_col):
@@ -68,6 +82,7 @@
         pl.semaphore_signal(
             barrier, inc=1, device_id={"row": lax.rem(my_row + d, n_row)}, device_id_type=MESH
         )
+    x_load.wait()
     pl.semaphore_wait(barrier, n_row + n_col - 2)
 
     row_copies = fan_col(lambda peer: x_ref, lambda d: row_x.at[my_col], rx_s, rx_r)
@@ -76,7 +91,8 @@
     row_x[my_col] = x_own
     col_x[my_row] = x_own
 
-    load.wait()
+    for copy in [*small_loads, load]:
+        copy.wait()
     for b in range(n_blk):
         high, low = halves(tiles[b])
         split[b] = jnp.concatenate([high, low], axis=1)
@@ -103,10 +119,6 @@
 
     x_wide = jnp.concatenate(row_two, axis=1)
     metric_part = fold(dot_nt(x_wide, x_wide))
-    met_out[...] = jnp.concatenate(
-        [metric_part, jnp.zeros((count, BLK - count), F32)], axis=1
-    )
-    met_copies = fan_row(lambda peer: met_out, lambda d: met_in.at[d], m_s, m_r)
 
     part_one = [jnp.zeros((count, BLK), F32) for _ in range(n_col)]
     for b in range(n_blk):
@@ -115,6 +127,11 @@
         place = rows_ref[0, b]
         for r in range(n_col):
             part_one[r] = part_one[r] + (place == r).astype(F32) * term
+        if b == n_blk // 4:
+            met_out[...] = jnp.concatenate(
+                [metric_part, jnp.zeros((count, BLK - count), F32)], axis=1
+            )
+            met_copies = fan_row(lambda peer: met_out, lambda d: met_in.at[d], m_s, m_r)
     for r in range(n_col):
         p1_out[r] = part_one[r]
     p1_copies = fan_col(lambda peer: p1_out.at[peer], lambda d: p1_in.at[d], p1_s, p1_r)
@@ -138,7 +155,21 @@
     g1_out[...] = jnp.concatenate(
         [jnp.sum(spread[g * per:(g + 1) * per], axis=0, keepdims=True) for g in range(groups)], axis=0
     )
-    g1_copies = fan_row(lambda peer: g1_out, lambda d: g1_in.at[d], g1_s, g1_r)
+    direct = n_row * n_col <= DIRECT
+    if direct:
+        g1_copies = []
+        for d in range(1, n_row * n_col):
+            peer = {"row": lax.rem(my_row + d // n_col, n_row), "col": lax.rem(my_col + d % n_col, n_col)}
+            g1_copies.append(
+                pltpu.make_async_remote_copy(
+                    src_ref=g1_out, dst_ref=g1_in.at[d], send_sem=g1_s.at[d], recv_sem=g1_r.at[d],
+                    device_id=peer, device_id_type=MESH,
+                )
+            )
+        for copy in g1_copies:
+            copy.start()
+    else:
+        g1_copies = fan_row(lambda peer: g1_out, lambda d: g1_in.at[d], g1_s, g1_r)
 
     part_two = [jnp.zeros((count, BLK), F32) for _ in range(n_row)]
     for b in range(n_blk):
@@ -151,13 +182,11 @@
         p2_out[q] = part_two[q]
     p2_copies = fan_row(lambda peer: p2_out.at[peer], lambda d: p2_in.at[d], p2_s, p2_r)
 
-    for copy in g1_copies:
-        copy.wait()
-    total = g1_out[...]
-    for d in range(1, n_row):
-        total = total + g1_in[d]
-    g2_out[...] = total
-    g2_copies = fan_col(lambda peer: g2_out, lambda d: g2_in.at[d], g2_s, g2_r)
+    if not direct:
+        for copy in g1_copies:
+            copy.wait()
+        g2_out[...] = add([g1_out[...]] + [g1_in[d] for d in range(1, n_row)])
+        g2_copies = fan_col(lambda peer: g2_out, lambda d: g2_in.at[d], g2_s, g2_r)
 
     for copy in met_copies:
         copy.wait()
@@ -187,22 +216,26 @@
         image = image + p2_in[d]
     for copy in p1_copies:
         copy.wait()
-    image = image + p1_out[my_col]
-    for d in range(1, n_col):
-        image = image + p1_in[d]
-    image_ref[...] = image
-
-    for copy in g2_copies:
-        copy.wait()
-    gram = g2_out[...]
-    for d in range(1, n_col):
-        gram = gram + g2_in[d]
+    image = add([image, p1_out[my_col]] + [p1_in[d] for d in range(1, n_col)])
+    out_ref[0] = image
+
+    for copy in g1_copies if direct else g2_copies:
+        copy.wait()
+    if direct:
+        gram = add([g1_out[...]] + [g1_in[d] for d in range(1, n_row * n_col)])
+    else:
+        gram = add([g2_out[...]] + [g2_in[d] for d in range(1, n_col)])
     wide = jnp.concatenate(
         [jnp.broadcast_to(gram[g:g + 1], (per, BLK)) for g in range(groups)], axis=0
     )
     wide = jnp.where(keep, wide, 0.0)
     o = dot_nn(jnp.concatenate(halves(wide), axis=0), y_two)
-    resid_ref[...] = image - (o[:count, :BLK] + o[count:, :BLK] + o[:count, BLK:])
+    out_ref[1] = image - (o[:count, :BLK] + o[count:, :BLK] + o[:count, BLK:])
+
+
+def part_kernel(both_ref, image_ref, resid_ref):
+    image_ref[...] = both_ref[0]
+    resid_ref[...] = both_ref[1]
 
 
 def per_device(n_row, n_col, vectors, diag_energy, blocks, block_row, block_col):
@@ -210,15 +243,19 @@
     n_blk = blocks.shape[1]
     groups = count // 8
     piece = (count, BLK)
+    n_all = n_row * n_col if n_row * n_col <= DIRECT else n_row
     vmem = pl.BlockSpec(memory_space=pltpu.VMEM)
-    smem = pl.BlockSpec(memory_space=pltpu.SMEM)
     dma = pltpu.SemaphoreType.DMA
-    return pl.pallas_call(
+    both = pl.pallas_call(
         functools.partial(kernel, n_row, n_col),
-        out_shape=[jax.ShapeDtypeStruct(piece, F32)] * 2,
-        in_specs=[vmem, vmem, smem, smem, pl.BlockSpec(memory_space=pl.ANY)],
-        out_specs=[vmem, vmem],
+        out_shape=pltpu.VMEM((2,) + piece, F32),
+        in_specs=[pl.BlockSpec(memory_space=pl.ANY)] * 5,
+        out_specs=vmem,
         scratch_shapes=[
+            pltpu.VMEM(piece, F32),
+            pltpu.VMEM((1, BLK), F32),
+            pltpu.SMEM((1, n_blk), jnp.int32),
+            pltpu.SMEM((1, n_blk), jnp.int32),
             pltpu.VMEM((n_blk, BLK, BLK), F32),
             pltpu.VMEM((n_blk, BLK, 2 * BLK), BF16),
             pltpu.VMEM((n_row,) + piece, F32),
@@ -232,20 +269,26 @@
             pltpu.VMEM((n_row,) + piece, F32),
             pltpu.VMEM((n_row,) + piece, F32),
             pltpu.VMEM((groups, BLK), F32),
-            pltpu.VMEM((n_row, groups, BLK), F32),
+            pltpu.VMEM((n_all, groups, BLK), F32),
             pltpu.VMEM((groups, BLK), F32),
             pltpu.VMEM((n_col, groups, BLK), F32),
-            dma,
+            dma((5,)),
             dma((n_row,)), dma((n_row,)),
             dma((n_col,)), dma((n_col,)),
             dma((n_row,)), dma((n_row,)),
             dma((n_col,)), dma((n_col,)),
             dma((n_row,)), dma((n_row,)),
-            dma((n_row,)), dma((n_row,)),
+            dma((n_all,)), dma((n_all,)),
             dma((n_col,)), dma((n_col,)),
         ],
         compiler_params=pltpu.CompilerParams(collective_id=0, has_side_effects=True),
     )(vectors, diag_energy.reshape(1, -1), block_row, block_col, blocks)
+    return pl.pallas_call(
+        part_kernel,
+        out_shape=[jax.ShapeDtypeStruct(piece, F32)] * 2,
+        in_specs=[vmem],
+        out_specs=[vmem, vmem],
+    )(pltpu.with_memory_space_constraint(both, pltpu.VMEM))
 
 
 def solution(mesh):

time: 24.5 us -> 19.6 us (0.80)
  local copies, waits for them, and re-layouts: 2.59 us -> 0 us
  Pallas kernels: 20.9 us -> 18.8 us
    unnamed x2 -> x0, local copies, waits for them, and re-layouts: 2.59 us -> none
    pallas_call x1 -> x2, Pallas kernels: 20.9 us -> 18.8 us  [the longest x1 18.2 us: per_device(): pl.pallas_call(functools.partial(kernel, n_row, n_col), out_shape=pltpu.V...]
where the time goes in v2:
time: 19.6 us; the launch traced here: 19.4 us
  Pallas kernels  18.8 us (96%)
  between operations  0.64 us (3%)
    pallas_call x1, Pallas kernels, per_device(): pl.pallas_call(functools.partial(kernel, n_row, n_col), out_shape=pltpu.V...  18.2 us
    pallas_call x1, Pallas kernels, per_device(): pl.pallas_call(part_kernel, out_shape=[jax.ShapeDtypeStruct(piece, F32)]...  0.61 us

profile of v2, /device:TPU:0, one launch (start us, length us, event | category | flops | bytes accessed | tf_op | source)
XLA Modules:
  0.0 19.4 jit_solution(18372964268819960769)
XLA Ops:
  0.6 18.2 %shard_map.68.both_ref = f32[2,16,128]{2,1,0:T(8,128)S(1)} custom-call(f32[16,128]{1,0:T(8,128)} %x_hbm.1, f32[1,128]{1,0:T(1,128)} %bitcast.1, s32[1,24]{1,0:T(1,128)} %rows_hbm.1, s32[1,24]{1,0:T(1,128)} %cols_hbm.1, f32[1,24,128,128]{3,2,1,0:T(8,128)} %blocks_hbm.1), custom_call_target="tpu_custom_call" | custom-call | tf_op jit(solution)/shard_map/pallas_call | solution.py:249
  18.8 0.6 %shard_map.69 = (f32[16,128]{1,0:T(8,128)}, f32[16,128]{1,0:T(8,128)}) custom-call(f32[2,16,128]{2,1,0:T(8,128)S(1)} %shard_map.68.both_ref), custom_call_target="tpu_custom_call" | custom-call | tf_op jit(solution)/shard_map/pallas_call | solution.py:286

commit v3 on v2

--- a/solution.py
+++ b/solution.py
@@ -97,28 +97,40 @@
         high, low = halves(tiles[b])
         split[b] = jnp.concatenate([high, low], axis=1)
 
+    per = BLK // count
+    groups = count // 8
+    lane = lax.broadcasted_iota(jnp.int32, (count, BLK), 1)
+    sub = lax.broadcasted_iota(jnp.int32, (count, BLK), 0)
+    keep = (lane // count) == (sub % per)
+
+    def fold(o):
+        return o[:count, :count] + o[count:, :count] + o[:count, count:]
+
+    def pack(square):
+        spread = jnp.where(keep, jnp.concatenate([square] * per, axis=1), 0.0)
+        return jnp.concatenate(
+            [jnp.sum(spread[g * per:(g + 1) * per], axis=0, keepdims=True) for g in range(groups)], axis=0
+        )
+
+    def unpack(packed):
+        wide = jnp.concatenate(
+            [jnp.broadcast_to(packed[g:g + 1], (per, BLK)) for g in range(groups)], axis=0
+        )
+        return jnp.where(keep, wide, 0.0)
+
     for copy in col_copies:
         copy.wait()
     zero = jnp.zeros((count, BLK), BF16)
+    col_two = []
     for q in range(n_row):
         high, low = halves(col_x[q])
         col_lhs[q] = jnp.concatenate(
             [jnp.concatenate([high, high], axis=1), jnp.concatenate([low, zero], axis=1)], axis=0
         )
-    for copy in row_copies:
-        copy.wait()
-    row_two = []
-    for r in range(n_col):
-        high, low = halves(row_x[r])
-        both = jnp.concatenate([high, low], axis=0)
-        row_lhs[r] = both
-        row_two.append(both)
-
-    def fold(o):
-        return o[:count, :count] + o[count:, :count] + o[:count, count:]
-
-    x_wide = jnp.concatenate(row_two, axis=1)
-    metric_part = fold(dot_nt(x_wide, x_wide))
+        col_two.append(jnp.concatenate([high, low], axis=0))
+    x_wide = jnp.concatenate(col_two, axis=1)
+    met_out[...] = pack(fold(dot_nt(x_wide, x_wide)))
+    met_copies = fan_col(lambda peer: met_out, lambda d: met_in.at[d], m_s, m_r)
 
     part_one = [jnp.zeros((count, BLK), F32) for _ in range(n_col)]
     for b in range(n_blk):
@@ -127,11 +139,6 @@
         place = rows_ref[0, b]
         for r in range(n_col):
             part_one[r] = part_one[r] + (place == r).astype(F32) * term
-        if b == n_blk // 4:
-            met_out[...] = jnp.concatenate(
-                [metric_part, jnp.zeros((count, BLK - count), F32)], axis=1
-            )
-            met_copies = fan_row(lambda peer: met_out, lambda d: met_in.at[d], m_s, m_r)
     for r in range(n_col):
         p1_out[r] = part_one[r]
     p1_copies = fan_col(lambda peer: p1_out.at[peer], lambda d: p1_in.at[d], p1_s, p1_r)
@@ -140,21 +147,21 @@
     p_two = [jnp.concatenate(halves(p), axis=0) for p in part_one]
     x_two = jnp.concatenate(halves(x_own), axis=0)
     d_two = jnp.concatenate(halves(own_diag), axis=0)
+
+    for copy in row_copies:
+        copy.wait()
+    row_two = []
+    for r in range(n_col):
+        both = jnp.concatenate(halves(row_x[r]), axis=0)
+        row_lhs[r] = both
+        row_two.append(both)
     gram_part = fold(
         dot_nt(
             jnp.concatenate(row_two + p_two + [x_two], axis=1),
             jnp.concatenate(p_two + row_two + [d_two], axis=1),
         )
     )
-    per = BLK // count
-    groups = count // 8
-    lane = lax.broadcasted_iota(jnp.int32, (count, BLK), 1)
-    sub = lax.broadcasted_iota(jnp.int32, (count, BLK), 0)
-    keep = (lane // count) == (sub % per)
-    spread = jnp.where(keep, jnp.concatenate([gram_part] * per, axis=1), 0.0)
-    g1_out[...] = jnp.concatenate(
-        [jnp.sum(spread[g * per:(g + 1) * per], axis=0, keepdims=True) for g in range(groups)], axis=0
-    )
+    g1_out[...] = pack(gram_part)
     direct = n_row * n_col <= DIRECT
     if direct:
         g1_copies = []
@@ -190,21 +197,22 @@
 
     for copy in met_copies:
         copy.wait()
-    metric = met_out[...]
-    for d in range(1, n_row):
-        metric = metric + met_in[d]
+    metric = unpack(add([met_out[...]] + [met_in[d] for d in range(1, n_col)]))
+    shift = count
+    while shift < BLK:
+        metric = metric + pltpu.roll(metric, shift, 1)
+        shift *= 2
+    lines = [jnp.broadcast_to(metric[:, k:k + 1], (count, BLK)) for k in range(count)]
     solved = x_own
+    pivots = jnp.ones((count, BLK), F32)
     for k in range(count):
-        ratio = jnp.where(
-            sub == k, 0.0,
-            jnp.broadcast_to(metric[:, k:k + 1], (count, BLK))
-            / jnp.broadcast_to(metric[k:k + 1, k:k + 1], (count, BLK)),
-        )
+        pivot = lines[k][k:k + 1]
+        pivots = jnp.where(sub == k, pivot, pivots)
+        ratio = jnp.where(sub == k, 0.0, lines[k] / pivot)
         solved = solved - ratio * solved[k:k + 1]
-        metric = metric - ratio * metric[k:k + 1]
-    pivots = jnp.sum(jnp.where(lane == sub, metric, 0.0), axis=1, keepdims=True)
-    solved = solved / pivots
-    high, low = halves(solved)
+        for j in range(k + 1, count):
+            lines[j] = lines[j] - ratio * lines[j][k:k + 1]
+    high, low = halves(solved / pivots)
     y_two = jnp.concatenate(
         [jnp.concatenate([high] * per, axis=0), jnp.concatenate([low] * per, axis=0)], axis=1
     )
@@ -225,10 +233,7 @@
         gram = add([g1_out[...]] + [g1_in[d] for d in range(1, n_row * n_col)])
     else:
         gram = add([g2_out[...]] + [g2_in[d] for d in range(1, n_col)])
-    wide = jnp.concatenate(
-        [jnp.broadcast_to(gram[g:g + 1], (per, BLK)) for g in range(groups)], axis=0
-    )
-    wide = jnp.where(keep, wide, 0.0)
+    wide = unpack(gram)
     o = dot_nn(jnp.concatenate(halves(wide), axis=0), y_two)
     out_ref[1] = image - (o[:count, :BLK] + o[count:, :BLK] + o[:count, BLK:])
 
@@ -262,8 +267,8 @@
             pltpu.VMEM((n_col,) + piece, F32),
             pltpu.VMEM((n_row, 2 * count, 2 * BLK), BF16),
             pltpu.VMEM((n_col, 2 * count, BLK), BF16),
-            pltpu.VMEM(piece, F32),
-            pltpu.VMEM((n_row,) + piece, F32),
+            pltpu.VMEM((groups, BLK), F32),
+            pltpu.VMEM((n_col, groups, BLK), F32),
             pltpu.VMEM((n_col,) + piece, F32),
             pltpu.VMEM((n_col,) + piece, F32),
             pltpu.VMEM((n_row,) + piece, F32),
@@ -275,7 +280,7 @@
             dma((5,)),
             dma((n_row,)), dma((n_row,)),
             dma((n_col,)), dma((n_col,)),
-            dma((n_row,)), dma((n_row,)),
+            dma((n_col,)), dma((n_col,)),
             dma((n_col,)), dma((n_col,)),
             dma((n_row,)), dma((n_row,)),
             dma((n_all,)), dma((n_all,)),

time: 19.6 us -> 18.8 us (0.959)
  Pallas kernels: 18.8 us -> 17.9 us
    pallas_call x1, Pallas kernels: 18.2 us -> 17.3 us  [per_device(): pl.pallas_call(functools.partial(kernel, n_row, n_col), out_shape=pltpu.V...]
where the time goes in v3:
time: 18.8 us; the launch traced here: 18.6 us
  Pallas kernels  17.9 us (95%)
  between operations  0.64 us (3%)
    pallas_call x1, Pallas kernels, per_device(): pl.pallas_call(functools.partial(kernel, n_row, n_col), out_shape=pltpu.V...  17.3 us
    pallas_call x1, Pallas kernels, per_device(): pl.pallas_call(part_kernel, out_shape=[jax.ShapeDtypeStruct(piece, F32)]...  0.61 us

profile of v3, /device:TPU:0, one launch (start us, length us, event | category | flops | bytes accessed | tf_op | source)
XLA Modules:
  0.0 18.6 jit_solution(15434557024250641008)
XLA Ops:
  0.6 17.3 %shard_map.68.both_ref = f32[2,16,128]{2,1,0:T(8,128)S(1)} custom-call(f32[16,128]{1,0:T(8,128)} %x_hbm.1, f32[1,128]{1,0:T(1,128)} %bitcast.1, s32[1,24]{1,0:T(1,128)} %rows_hbm.1, s32[1,24]{1,0:T(1,128)} %cols_hbm.1, f32[1,24,128,128]{3,2,1,0:T(8,128)} %blocks_hbm.1), custom_call_target="tpu_custom_call" | custom-call | tf_op jit(solution)/shard_map/pallas_call | solution.py:254
  18.0 0.6 %shard_map.69 = (f32[16,128]{1,0:T(8,128)}, f32[16,128]{1,0:T(8,128)}) custom-call(f32[2,16,128]{2,1,0:T(8,128)S(1)} %shard_map.68.both_ref), custom_call_target="tpu_custom_call" | custom-call | tf_op jit(solution)/shard_map/pallas_call | solution.py:291

commit v4 on v3

--- a/solution.py
+++ b/solution.py
@@ -144,35 +144,40 @@
     p1_copies = fan_col(lambda peer: p1_out.at[peer], lambda d: p1_in.at[d], p1_s, p1_r)
 
     own_diag = diag_ref[...] * x_own
-    p_two = [jnp.concatenate(halves(p), axis=0) for p in part_one]
     x_two = jnp.concatenate(halves(x_own), axis=0)
     d_two = jnp.concatenate(halves(own_diag), axis=0)
 
-    for copy in row_copies:
-        copy.wait()
-    row_two = []
-    for r in range(n_col):
-        both = jnp.concatenate(halves(row_x[r]), axis=0)
-        row_lhs[r] = both
-        row_two.append(both)
-    gram_part = fold(
-        dot_nt(
-            jnp.concatenate(row_two + p_two + [x_two], axis=1),
-            jnp.concatenate(p_two + row_two + [d_two], axis=1),
-        )
-    )
+    sum_two = dot_nt(x_two, d_two)
+
+    def take(at, both):
+        row_lhs[at] = both
+        p_here = jnp.concatenate(halves(p1_out[at]), axis=0)
+        return dot_nt(jnp.concatenate([both, p_here], axis=1), jnp.concatenate([p_here, both], axis=1))
+
+    sum_two = sum_two + take(my_col, x_two)
+    for d in range(1, n_col):
+        row_copies[d - 1].wait()
+        at = lax.rem(my_col - d + n_col, n_col)
+        sum_two = sum_two + take(at, jnp.concatenate(halves(row_x[at]), axis=0))
+    gram_part = fold(sum_two)
     g1_out[...] = pack(gram_part)
     direct = n_row * n_col <= DIRECT
     if direct:
         g1_copies = []
-        for d in range(1, n_row * n_col):
-            peer = {"row": lax.rem(my_row + d // n_col, n_row), "col": lax.rem(my_col + d % n_col, n_col)}
-            g1_copies.append(
-                pltpu.make_async_remote_copy(
-                    src_ref=g1_out, dst_ref=g1_in.at[d], send_sem=g1_s.at[d], recv_sem=g1_r.at[d],
-                    device_id=peer, device_id_type=MESH,
+        upper = my_col // (n_col // 2)
+        for at in range(1, n_col + 1):
+            for over in sorted(range(n_row), key=lambda o: abs(2 * o - n_row)):
+                if at == n_col and over == 0:
+                    continue
+                far = lax.rem(upper * at + (1 - upper) * (n_col - at), n_col)
+                slot = over * n_col + far
+                peer = {"row": lax.rem(my_row + over, n_row), "col": lax.rem(my_col + far, n_col)}
+                g1_copies.append(
+                    pltpu.make_async_remote_copy(
+                        src_ref=g1_out, dst_ref=g1_in.at[slot], send_sem=g1_s.at[slot],
+                        recv_sem=g1_r.at[slot], device_id=peer, device_id_type=MESH,
+                    )
                 )
-            )
         for copy in g1_copies:
             copy.start()
     else:

time: 18.8 us -> 18.6 us (0.989)
  Pallas kernels: 17.9 us -> 17.7 us
    pallas_call x1, Pallas kernels: 17.3 us -> 17.1 us  [per_device(): pl.pallas_call(functools.partial(kernel, n_row, n_col), out_shape=pltpu.V...]
where the time goes in v4:
time: 18.6 us; the launch traced here: 18.4 us
  Pallas kernels  17.7 us (95%)
  between operations  0.64 us (3%)
    pallas_call x1, Pallas kernels, per_device(): pl.pallas_call(functools.partial(kernel, n_row, n_col), out_shape=pltpu.V...  17.1 us
    pallas_call x1, Pallas kernels, per_device(): pl.pallas_call(part_kernel, out_shape=[jax.ShapeDtypeStruct(piece, F32)]...  0.61 us

profile of v4, /device:TPU:0, one launch (start us, length us, event | category | flops | bytes accessed | tf_op | source)
XLA Modules:
  0.0 18.4 jit_solution(10349370241486814708)
XLA Ops:
  0.6 17.1 %shard_map.68.both_ref = f32[2,16,128]{2,1,0:T(8,128)S(1)} custom-call(f32[16,128]{1,0:T(8,128)} %x_hbm.1, f32[1,128]{1,0:T(1,128)} %bitcast.1, s32[1,24]{1,0:T(1,128)} %rows_hbm.1, s32[1,24]{1,0:T(1,128)} %cols_hbm.1, f32[1,24,128,128]{3,2,1,0:T(8,128)} %blocks_hbm.1), custom_call_target="tpu_custom_call" | custom-call | tf_op jit(solution)/shard_map/pallas_call | solution.py:259
  17.8 0.6 %shard_map.69 = (f32[16,128]{1,0:T(8,128)}, f32[16,128]{1,0:T(8,128)}) custom-call(f32[2,16,128]{2,1,0:T(8,128)S(1)} %shard_map.68.both_ref), custom_call_target="tpu_custom_call" | custom-call | tf_op jit(solution)/shard_map/pallas_call | solution.py:296

commit v5 on v4

--- a/solution.py
+++ b/solution.py
@@ -85,7 +85,18 @@
     x_load.wait()
     pl.semaphore_wait(barrier, n_row + n_col - 2)
 
-    row_copies = fan_col(lambda peer: x_ref, lambda d: row_x.at[my_col], rx_s, rx_r)
+    upper = my_col // (n_col // 2)
+    row_copies = []
+    for at in range(1, n_col):
+        far = upper * at + (1 - upper) * (n_col - at)
+        row_copies.append(
+            pltpu.make_async_remote_copy(
+                src_ref=x_ref, dst_ref=row_x.at[my_col], send_sem=rx_s.at[far], recv_sem=rx_r.at[far],
+                device_id={"col": lax.rem(my_col + far, n_col)}, device_id_type=MESH,
+            )
+        )
+    for copy in row_copies:
+        copy.start()
     col_copies = fan_row(lambda peer: x_ref, lambda d: col_x.at[my_row], cx_s, cx_r)
     x_own = x_ref[...]
     row_x[my_col] = x_own
@@ -155,16 +166,16 @@
         return dot_nt(jnp.concatenate([both, p_here], axis=1), jnp.concatenate([p_here, both], axis=1))
 
     sum_two = sum_two + take(my_col, x_two)
-    for d in range(1, n_col):
-        row_copies[d - 1].wait()
-        at = lax.rem(my_col - d + n_col, n_col)
+    for copy_at in range(1, n_col):
+        row_copies[copy_at - 1].wait()
+        far = upper * copy_at + (1 - upper) * (n_col - copy_at)
+        at = lax.rem(my_col - far + n_col, n_col)
         sum_two = sum_two + take(at, jnp.concatenate(halves(row_x[at]), axis=0))
     gram_part = fold(sum_two)
     g1_out[...] = pack(gram_part)
     direct = n_row * n_col <= DIRECT
     if direct:
         g1_copies = []
-        upper = my_col // (n_col // 2)
         for at in range(1, n_col + 1):
             for over in sorted(range(n_row), key=lambda o: abs(2 * o - n_row)):
                 if at == n_col and over == 0:

time: 18.6 us -> 18.2 us (0.978)
  Pallas kernels: 17.7 us -> 17.3 us
    pallas_call x1, Pallas kernels: 17.1 us -> 16.7 us  [per_device(): pl.pallas_call(functools.partial(kernel, n_row, n_col), out_shape=pltpu.V...]
where the time goes in v5:
time: 18.2 us; the launch traced here: 18 us
  Pallas kernels  17.3 us (95%)
  between operations  0.64 us (4%)
    pallas_call x1, Pallas kernels, per_device(): pl.pallas_call(functools.partial(kernel, n_row, n_col), out_shape=pltpu.V...  16.7 us
    pallas_call x1, Pallas kernels, per_device(): pl.pallas_call(part_kernel, out_shape=[jax.ShapeDtypeStruct(piece, F32)]...  0.61 us

profile of v5, /device:TPU:0, one launch (start us, length us, event | category | flops | bytes accessed | tf_op | source)
XLA Modules:
  0.0 18.0 jit_solution(9182599582614910705)
XLA Ops:
  0.6 16.7 %shard_map.68.both_ref = f32[2,16,128]{2,1,0:T(8,128)S(1)} custom-call(f32[16,128]{1,0:T(8,128)} %x_hbm.1, f32[1,128]{1,0:T(1,128)} %bitcast.1, s32[1,24]{1,0:T(1,128)} %rows_hbm.1, s32[1,24]{1,0:T(1,128)} %cols_hbm.1, f32[1,24,128,128]{3,2,1,0:T(8,128)} %blocks_hbm.1), custom_call_target="tpu_custom_call" | custom-call | tf_op jit(solution)/shard_map/pallas_call | solution.py:270
  17.4 0.6 %shard_map.69 = (f32[16,128]{1,0:T(8,128)}, f32[16,128]{1,0:T(8,128)}) custom-call(f32[2,16,128]{2,1,0:T(8,128)S(1)} %shard_map.68.both_ref), custom_call_target="tpu_custom_call" | custom-call | tf_op jit(solution)/shard_map/pallas_call | solution.py:307

commit v6 on v5

--- a/solution.py
+++ b/solution.py
@@ -63,6 +63,16 @@
     fan_row = functools.partial(fan, "row", n_row, my_row)
     fan_col = functools.partial(fan, "col", n_col, my_col)
 
+    barrier = pltpu.get_barrier_semaphore()
+    for d in range(1, n_col):
+        pl.semaphore_signal(
+            barrier, inc=1, device_id={"col": lax.rem(my_col + d, n_col)}, device_id_type=MESH
+        )
+    for d in range(1, n_row):
+        pl.semaphore_signal(
+            barrier, inc=1, device_id={"row": lax.rem(my_row + d, n_row)}, device_id_type=MESH
+        )
+
     x_load, *small_loads, load = [
         pltpu.make_async_copy(source, target, load_sem.at[at])
         for at, (source, target) in enumerate(
@@ -72,16 +82,6 @@
     ]
     for copy in [x_load, *small_loads, load]:
         copy.start()
-
-    barrier = pltpu.get_barrier_semaphore()
-    for d in range(1, n_col):
-        pl.semaphore_signal(
-            barrier, inc=1, device_id={"col": lax.rem(my_col + d, n_col)}, device_id_type=MESH
-        )
-    for d in range(1, n_row):
-        pl.semaphore_signal(
-            barrier, inc=1, device_id={"row": lax.rem(my_row + d, n_row)}, device_id_type=MESH
-        )
     x_load.wait()
     pl.semaphore_wait(barrier, n_row + n_col - 2)
 

time: 18.2 us -> 18.1 us (level)
  no operation moved by 1% of the time
where the time goes in v6:
time: 18.1 us; the launch traced here: 17.9 us
  Pallas kernels  17.3 us (96%)
  between operations  0.64 us (4%)
    pallas_call x1, Pallas kernels, per_device(): pl.pallas_call(functools.partial(kernel, n_row, n_col), out_shape=pltpu.V...  16.7 us
    pallas_call x1, Pallas kernels, per_device(): pl.pallas_call(part_kernel, out_shape=[jax.ShapeDtypeStruct(piece, F32)]...  0.61 us

profile of v6, /device:TPU:0, one launch (start us, length us, event | category | flops | bytes accessed | tf_op | source)
XLA Modules:
  0.0 17.9 jit_solution(3665340329916433962)
XLA Ops:
  0.6 16.7 %shard_map.68.both_ref = f32[2,16,128]{2,1,0:T(8,128)S(1)} custom-call(f32[16,128]{1,0:T(8,128)} %x_hbm.1, f32[1,128]{1,0:T(1,128)} %bitcast.1, s32[1,24]{1,0:T(1,128)} %rows_hbm.1, s32[1,24]{1,0:T(1,128)} %cols_hbm.1, f32[1,24,128,128]{3,2,1,0:T(8,128)} %blocks_hbm.1), custom_call_target="tpu_custom_call" | custom-call | tf_op jit(solution)/shard_map/pallas_call | solution.py:270
  17.3 0.6 %shard_map.69 = (f32[16,128]{1,0:T(8,128)}, f32[16,128]{1,0:T(8,128)}) custom-call(f32[2,16,128]{2,1,0:T(8,128)S(1)} %shard_map.68.both_ref), custom_call_target="tpu_custom_call" | custom-call | tf_op jit(solution)/shard_map/pallas_call | solution.py:307
